TPU v7x, 256 devices: a whole 4x4x8 slice. The times are simulated.
256 devices in a mesh: row: 8 (over y, core), col: 8 (over x, z_hi), rep: 4 (over z_lo).
Axes of the slice: x: 4, y: 4, z: 8 (z_hi: 2, z_lo: 4; z = z_hi * 4 + z_lo), core: 2. Of those that a mesh axis runs over, the one named last changes fastest.
Arguments:
- features: float32 [256, 32768], P('rep', ('col', 'row')), may hold values from -6 to 6
- weight: float32 [256, 256], replicated, may hold values from -0.375 to 0.375
- cotangent: float32 [256, 32768], P('rep', ('row', 'col')), may hold values from -6 to 6
- tile_values: float32 [10240, 128, 128], P(('row', 'col')), may hold values from -0.078125 to 0.078125
- tile_row: int32 [10240], P(('row', 'col')), may hold values from 0 to 31
- tile_col: int32 [10240], P(('row', 'col')), may hold values from 0 to 31
- tile_kind: int32 [10240], P(('row', 'col')), may hold values from 0 to 159
- tile_count: int32 [64], P(('row', 'col')), may hold values from 40 to 160, as said below
Outputs:
- output: float32 [256, 32768], P('rep', ('row', 'col'))
- input_grad: float32 [256, 32768], P('rep', ('col', 'row'))
- weight_grad: float32 [256, 256], P('rep')
Inputs may be any that keep to these rules, and one draw needn't show every extreme that they name: `tile_count`: a block's slots at or after its count are not part of the adjacency; some block uses all 160 slots. `tile_row`: slots may repeat a tile position; their tiles add. `tile_kind`: an index into the 160 stored tiles of the same block.
All inputs are finite; a program needn't handle non-finite values.
Results may differ from a plain program's by a relative error of at most 0.0001.
Values sent between devices are 32-bit elements; how exact they have to be, the bound alone decides.
No kernel may reach another device: no remote copies, remote signals or barrier semaphores. Data moves between devices by JAX's collectives and lax.ppermute only.
A program may use at most 128 MiB of HBM per device.

v0:
```python
import jax
import jax.numpy as jnp
from jax import lax
from jax.sharding import PartitionSpec as P


def tile_terms(source, values, from_tile, to_tile, tile_kinds, live_weight, dest_tiles, transposed):
    feat_width = source.shape[0]
    tile_edge = values.shape[1]
    tiled = source.reshape(feat_width, source.shape[1] // tile_edge, tile_edge)
    picked = jnp.take(tiled, from_tile, axis=1)
    chosen = jnp.take(values, tile_kinds, axis=0)
    if transposed:
        products = jnp.einsum("fga,gab->fgb", picked, chosen, precision=lax.Precision.HIGHEST)
    else:
        products = jnp.einsum("fgb,gab->fga", picked, chosen, precision=lax.Precision.HIGHEST)
    onehot = (to_tile[:, None] == jnp.arange(dest_tiles, dtype=jnp.int32)[None, :]).astype(
        jnp.float32
    )
    onehot = onehot * live_weight[:, None]
    spread = jnp.einsum("fgt,gd->fdt", products, onehot, precision=lax.Precision.HIGHEST)
    return spread.reshape(feat_width, dest_tiles * tile_edge)


def aggregate(source, values, from_tile, to_tile, tile_kinds, live_count, dest_tiles, transposed):
    slot_total = tile_kinds.shape[0]
    live_weight = (jnp.arange(slot_total, dtype=jnp.int32) < live_count).astype(jnp.float32)
    return tile_terms(
        source, values, from_tile, to_tile, tile_kinds, live_weight, dest_tiles, transposed
    )


def local(features, weight, cotangent, tile_values, tile_row, tile_col, tile_kind, tile_count):
    n_rowdev = lax.axis_size("row")
    n_coldev = lax.axis_size("col")
    n_repdev = lax.axis_size("rep")
    quarter = weight.shape[0] // n_repdev
    rep_index = lax.axis_index("rep")
    own_rows = lax.dynamic_slice_in_dim(weight, rep_index * quarter, quarter, 0)
    own_cols = lax.dynamic_slice_in_dim(weight, rep_index * quarter, quarter, 1)
    stretch_len = features.shape[1]
    tile_edge = tile_values.shape[1]
    live_count = tile_count[0]
    row_tiles = n_coldev * stretch_len // tile_edge
    col_tiles = n_rowdev * stretch_len // tile_edge
    mixed = lax.psum_scatter(
        lax.dot_general(
            own_rows,
            features,
            (((0,), (0,)), ((), ())),
            precision=lax.Precision.HIGHEST,
            preferred_element_type=jnp.float32,
        ),
        "rep",
        scatter_dimension=0,
        tiled=True,
    )
    column_block = lax.all_gather(mixed, "row", axis=1, tiled=True)
    partial_value = aggregate(
        column_block, tile_values, tile_col, tile_row, tile_kind, live_count, row_tiles, False
    )
    summed = lax.psum_scatter(partial_value, "col", scatter_dimension=1, tiled=True)
    output, pullback = jax.vjp(lambda v: jax.nn.gelu(v, approximate=True), summed)
    (grad_pre,) = pullback(cotangent)
    row_block = lax.all_gather(grad_pre, "col", axis=1, tiled=True)
    partial_back = aggregate(
        row_block, tile_values, tile_row, tile_col, tile_kind, live_count, col_tiles, True
    )
    grad_mixed = lax.psum_scatter(partial_back, "row", scatter_dimension=1, tiled=True)
    input_grad = lax.psum_scatter(
        jnp.dot(
            own_cols,
            grad_mixed,
            preferred_element_type=jnp.float32,
            precision=lax.Precision.HIGHEST,
        ),
        "rep",
        scatter_dimension=0,
        tiled=True,
    )
    weight_part = lax.dot_general(
        features,
        lax.all_gather(grad_mixed, "rep", axis=0, tiled=True),
        (((1,), (1,)), ((), ())),
        precision=lax.Precision.HIGHEST,
        preferred_element_type=jnp.float32,
    )
    node_total = stretch_len * n_rowdev * n_coldev
    weight_grad = lax.psum(weight_part * float(node_total) ** (-0.5), ("row", "col"))
    return (output, input_grad, weight_grad)


def solution(mesh):
    return jax.shard_map(
        local,
        mesh=mesh,
        in_specs=(
            P("rep", ("col", "row")),
            P(),
            P("rep", ("row", "col")),
            P(("row", "col"), None, None),
            P(("row", "col")),
            P(("row", "col")),
            P(("row", "col")),
            P(("row", "col")),
        ),
        out_specs=(P("rep", ("row", "col")), P("rep", ("col", "row")), P("rep", None)),
        check_vma=False,
    )
```

profile of v0, /device:TPU:2, one launch (start us, length us, event | category | flops | bytes accessed | tf_op | source)
XLA Modules:
  0.0 1082.4 jit_solution(2901445615518222513)
XLA Ops:
  8.1 2.3 fusion.39
  10.5 30.2 %reduce-scatter.5.cloned.1.call-done = f32[64,512]{1,0:T(8,128)} async-done(((f32[256,512]{1,0:T(8,128)}), f32[64,512]{1,0:T(8,128)}) %reduce-scatter.5.cloned.1.call-update) | async-done | bytes 131088 | tf_op jit(solution)/shard_map/reduce_scatter | solution.py:46
  42.1 14.2 %gather_fusion = f32[160,128,128]{2,1,0:T(8,128)} fusion(f32[160,128,128]{2,1,0:T(8,128)} %param.15, s32[1024]{0:T(1024)S(1)} %pad_clamp_fusion.2), kind=kCustom, calls=%fused_computation.clone | custom fusion | bytes 20972160 | tf_op jit(solution)/shard_map/jit(_take)/gather | solution.py:12
  56.3 10.5 all-gather.3.cloned.1.call-done
  66.8 1.3 copy_bitcast_fusion.3
  68.2 3.3 gather_fusion.1
  71.5 24.3 %fusion.20 = f32[64,160,128]{2,0,1:T(8,128)S(1)} fusion(f32[160,64,128]{2,1,0:T(8,128)} %gather_fusion.1, pred[160]{0:T(512)(128)(4,1)S(1)} %get-tuple-element.7, f32[160,128,128]{2,1,0:T(8,128)} %gather_fusion, pred[160]{0:T(512)(128)(4,1)S(1)} %get-tuple-element.8), kind=kOutput, calls=%fused_computation.23 | convolution fusion | flops 2017198080 | bytes 20971840 | tf_op jit(solution)/shard_map/fgb,gab->fga/dot_general | solution.py:16
  95.8 5.6 fusion.8
  101.5 1.6 copy.29
  103.1 87.2 %reduce-scatter.7.cloned.1.call-done = f32[64,512]{1,0:T(8,128)} async-done(((f32[64,4096]{1,0:T(8,128)}), f32[64,512]{1,0:T(8,128)}) %reduce-scatter.7.cloned.1.call-update) | async-done | bytes 131088 | tf_op jit(solution)/shard_map/reduce_scatter | solution.py:62
  190.4 1.7 fusion.36
  192.2 59.1 %all-gather.5.cloned.1.call-done = f32[64,4096]{1,0:T(8,128)} async-done(((f32[64,512]{1,0:T(8,128)}), f32[64,4096]{1,0:T(8,128)}) %all-gather.5.cloned.1.call-update) | async-done | bytes 1048592 | tf_op jit(solution)/shard_map/all_gather | solution.py:65
  251.3 1.3 copy_bitcast_fusion.2
  252.7 3.3 gather_fusion.2
  255.9 13.9 %fusion.25 = f32[64,160,128]{2,0,1:T(8,128)S(1)} fusion(f32[160,64,128]{2,1,0:T(8,128)} %gather_fusion.2, pred[160]{0:T(512)(128)(4,1)S(1)} %compare_and_fusion, f32[160,128,128]{2,1,0:T(8,128)} %gather_fusion, pred[160]{0:T(512)(128)(4,1)S(1)} %get-tuple-element.8), kind=kOutput, calls=%fused_computation.24 | convolution fusion | flops 2017198080 | bytes 20971840 | tf_op jit(solution)/shard_map/fga,gab->fgb/dot_general | solution.py:14
  269.8 5.6 fusion.6
  275.5 1.6 copy.28
  277.1 30.8 %reduce-scatter.9.cloned.1.call-done = f32[64,512]{1,0:T(8,128)} async-done(((f32[64,4096]{1,0:T(8,128)}), f32[64,512]{1,0:T(8,128)}) %reduce-scatter.9.cloned.1.call-update) | async-done | bytes 131088 | tf_op jit(solution)/shard_map/reduce_scatter | solution.py:69
  307.9 16.4 %all_gather.11 = f32[256,512]{1,0:T(8,128)S(1)} all-gather(f32[64,512]{1,0:T(8,128)} %reduce-scatter.9.cloned.1.call-done), channel_id=1, replica_groups=mesh['row'=8,'col'=8,'rep'=4] {'rep'}, dimensions={0}, use_global_device_ids=true | all-gather | bytes 655360 | tf_op jit(solution)/shard_map/all_gather | solution.py:83
  324.4 1.2 fusion.30
  325.7 2.3 fusion.37
  328.0 722.2 %all-reduce.2.cloned.1.call-done = f32[64,256]{1,0:T(8,128)} async-done(((f32[64,256]{1,0:T(8,128)}), f32[64,256]{1,0:T(8,128)}) %all-reduce.2.cloned.1.call-update) | async-done | bytes 65552 | tf_op jit(solution)/shard_map/psum | solution.py:89
  1050.2 23.9 %reduce-scatter.11.cloned.1.call-done = f32[64,512]{1,0:T(8,128)} async-done(((f32[256,512]{1,0:T(8,128)}), f32[64,512]{1,0:T(8,128)}) %reduce-scatter.11.cloned.1.call-update) | async-done | bytes 131088 | tf_op jit(solution)/shard_map/reduce_scatter | solution.py:70
  1074.1 1.5 copy.32
  (35 shorter events, 2.1 us)
Async XLA Ops:
  7.2 1.0 copy-start
  7.2 33.5 %reduce-scatter.5.cloned.1.call-start = ((), (), s32[]{:S(2)}) async-start(), calls=%async_computation.4 | async-start | bytes 655360 | tf_op jit(solution)/shard_map/reduce_scatter | solution.py:46
  10.5 56.4 %all-gather.3.cloned.1.call-start = ((), (), s32[]{:S(2)}) async-start(), calls=%async_computation.5 | async-start | bytes 1179648 | tf_op jit(solution)/shard_map/all_gather | solution.py:58
  40.7 149.7 %reduce-scatter.7.cloned.1.call-start = ((), (), s32[]{:S(2)}) async-start(), calls=%async_computation.6 | async-start | bytes 1179648 | tf_op jit(solution)/shard_map/reduce_scatter | solution.py:62
  42.1 14.2 %copy-start.3 = (s32[160]{0:T(256)S(1)}, s32[160]{0:T(256)}, u32[]{:S(2)}) copy-start(s32[160]{0:T(256)} %param.17) | copy-start | bytes 1924
  42.1 14.2 %copy-start.5 = (s32[160]{0:T(256)S(1)}, s32[160]{0:T(256)}, u32[]{:S(2)}) copy-start(s32[160]{0:T(256)} %param.18) | copy-start | bytes 1924
  71.5 24.3 %copy-start.4 = (s32[160]{0:T(256)S(1)}, s32[160]{0:T(256)}, u32[]{:S(2)}) copy-start(s32[160]{0:T(256)} %param.16) | copy-start | bytes 1924
  95.8 94.6 %copy-start.2 = (f32[64,512]{1,0:T(8,128)S(1)}, f32[64,512]{1,0:T(8,128)}, u32[]{:S(2)}) copy-start(f32[64,512]{1,0:T(8,128)} %param.14) | copy-start | bytes 393220
  103.1 148.2 %all-gather.5.cloned.1.call-start = ((), (), s32[]{:S(2)}) async-start(), calls=%async_computation.7 | async-start | bytes 1179648 | tf_op jit(solution)/shard_map/all_gather | solution.py:65
  192.1 115.8 %reduce-scatter.9.cloned.1.call-start = ((), (), s32[]{:S(2)}) async-start(), calls=%async_computation.8 | async-start | bytes 1179648 | tf_op jit(solution)/shard_map/reduce_scatter | solution.py:69
  269.8 54.5 %copy-start.1 = (f32[64,512]{1,0:T(8,128)S(1)}, f32[64,512]{1,0:T(8,128)}, u32[]{:S(2)}) copy-start(f32[64,512]{1,0:T(8,128)} %param.12) | copy-start | bytes 393220
  277.1 773.1 %all-reduce.2.cloned.1.call-start = ((), (), s32[]{:S(2)}) async-start(), calls=%async_computation.10 | async-start | bytes 131072 | tf_op jit(solution)/shard_map/psum | solution.py:89
  325.6 748.5 %reduce-scatter.11.cloned.1.call-start = ((), (), s32[]{:S(2)}) async-start(), calls=%async_computation.9 | async-start | bytes 655360 | tf_op jit(solution)/shard_map/reduce_scatter | solution.py:70
Sparse Core Ops, SparseCore 0:
  10.6 30.0 reduce-scatter.4
  42.5 24.2 all-gather.2
  103.2 87.1 reduce-scatter.6
  193.4 57.8 all-gather.4
  277.2 30.6 reduce-scatter.8
  325.7 724.4 all-reduce.1
  1053.3 20.7 reduce-scatter.10
where the time goes:
time: 1080 us
  waiting for transfers between devices  964 us (89%)
  matrix products  55.3 us (5%)
  local copies, waits for them, and re-layouts  29 us (3%)
  blocking collectives  16.4 us (2%)
  between operations  14.9 us (1%)
    psum x1, waiting for transfers between devices, local(): lax.psum(weight_part * float(node_total) ** (-0.5), ('row', 'col'))  722 us
    reduce_scatter x1, waiting for transfers between devices, local(): lax.psum_scatter(partial_value, 'col', scatter_dimension=1, tiled=True)  87.2 us
    all_gather x1, waiting for transfers between devices, local(): row_block = lax.all_gather(grad_pre, 'col', axis=1, tiled=True)  59.1 us
    reduce_scatter x1, waiting for transfers between devices, local(): lax.psum_scatter(partial_back, 'row', scatter_dimension=1, tiled=True)  30.8 us
    reduce_scatter x1, waiting for transfers between devices, local(): lax.psum_scatter(lax.dot_general(own_rows, features, (((0,), (0,)), ((),...  30.2 us
    dot_general x1, matrix products, tile_terms(): jnp.einsum('fgb,gab->fga', picked, chosen, precision=lax.Precision.HIGHEST)  24.3 us
    reduce_scatter x1, waiting for transfers between devices, local(): lax.psum_scatter(jnp.dot(own_cols, grad_mixed, preferred_element_type=jnp...  23.9 us
  transfers between devices with their start and end apart: 7, of which 7 were waited for; matrix products, arithmetic and copies ran while one was open for 2% of the time, Pallas kernels for 0%

commit v1 on v0

--- a/solution.py
+++ b/solution.py
@@ -86,7 +86,9 @@
         preferred_element_type=jnp.float32,
     )
     node_total = stretch_len * n_rowdev * n_coldev
-    weight_grad = lax.psum(weight_part * float(node_total) ** (-0.5), ("row", "col"))
+    weight_grad = jax.lax.psum(
+        jax.lax.psum(weight_part * float(node_total) ** (-0.5), "col"), "row"
+    )
     return (output, input_grad, weight_grad)
 
 

time: 1080 us -> 529 us (0.49)
  waiting for transfers between devices: 964 us -> 411 us
    psum x1 -> x2, waiting for transfers between devices: 722 us -> 163 us  [the longest x1 102 us: local(): jax.lax.psum(weight_part * float(node_total) ** (-0.5), 'col')]
  transfers between devices with their start and end apart: 7 -> 8, of which waited for: 7 -> 8; matrix products, arithmetic and copies ran while one was open for 2% -> 3% of each run, Pallas kernels for 0% -> 0%
where the time goes in v1:
time: 529 us
  waiting for transfers between devices  411 us (78%)
  matrix products  55.3 us (10%)
  local copies, waits for them, and re-layouts  29 us (5%)
  blocking collectives  16.4 us (3%)
  between operations  14.9 us (3%)
    psum x1, waiting for transfers between devices, local(): jax.lax.psum(weight_part * float(node_total) ** (-0.5), 'col')  102 us
    reduce_scatter x1, waiting for transfers between devices, local(): lax.psum_scatter(partial_value, 'col', scatter_dimension=1, tiled=True)  87.2 us
    psum x1, waiting for transfers between devices, local(): jax.lax.psum(jax.lax.psum(weight_part * float(node_total) ** (-0.5), 'col...  61 us
    all_gather x1, waiting for transfers between devices, local(): row_block = lax.all_gather(grad_pre, 'col', axis=1, tiled=True)  59.1 us
    reduce_scatter x1, waiting for transfers between devices, local(): lax.psum_scatter(partial_back, 'row', scatter_dimension=1, tiled=True)  30.8 us
    reduce_scatter x1, waiting for transfers between devices, local(): lax.psum_scatter(lax.dot_general(own_rows, features, (((0,), (0,)), ((),...  30.2 us
    reduce_scatter x1, waiting for transfers between devices, local(): lax.psum_scatter(jnp.dot(own_cols, grad_mixed, preferred_element_type=jnp...  29.2 us
    dot_general x1, matrix products, tile_terms(): jnp.einsum('fgb,gab->fga', picked, chosen, precision=lax.Precision.HIGHEST)  24.3 us
  transfers between devices with their start and end apart: 8, of which 8 were waited for; matrix products, arithmetic and copies ran while one was open for 3% of the time, Pallas kernels for 0%

profile of v1, /device:TPU:2, one launch (start us, length us, event | category | flops | bytes accessed | tf_op | source)
XLA Modules:
  0.0 529.0 jit_solution(12148352572495384220)
XLA Ops:
  8.1 2.3 fusion.39
  10.5 30.2 %reduce-scatter.5.cloned.1.call-done = f32[64,512]{1,0:T(8,128)} async-done(((f32[256,512]{1,0:T(8,128)}), f32[64,512]{1,0:T(8,128)}) %reduce-scatter.5.cloned.1.call-update) | async-done | bytes 131088 | tf_op jit(solution)/shard_map/reduce_scatter | solution.py:46
  42.1 14.2 %gather_fusion = f32[160,128,128]{2,1,0:T(8,128)} fusion(f32[160,128,128]{2,1,0:T(8,128)} %param.15, s32[1024]{0:T(1024)S(1)} %pad_clamp_fusion.2), kind=kCustom, calls=%fused_computation.clone | custom fusion | bytes 20972160 | tf_op jit(solution)/shard_map/jit(_take)/gather | solution.py:12
  56.3 10.5 %all-gather.3.cloned.1.call-done = f32[64,4096]{1,0:T(8,128)} async-done(((f32[64,512]{1,0:T(8,128)}), f32[64,4096]{1,0:T(8,128)}) %all-gather.3.cloned.1.call-update) | async-done | bytes 1048592 | tf_op jit(solution)/shard_map/all_gather | solution.py:58
  66.8 1.3 copy_bitcast_fusion.3
  68.2 3.3 gather_fusion.1
  71.5 24.3 %fusion.20 = f32[64,160,128]{2,0,1:T(8,128)S(1)} fusion(f32[160,64,128]{2,1,0:T(8,128)} %gather_fusion.1, pred[160]{0:T(512)(128)(4,1)S(1)} %get-tuple-element.7, f32[160,128,128]{2,1,0:T(8,128)} %gather_fusion, pred[160]{0:T(512)(128)(4,1)S(1)} %get-tuple-element.8), kind=kOutput, calls=%fused_computation.23 | convolution fusion | flops 2017198080 | bytes 20971840 | tf_op jit(solution)/shard_map/fgb,gab->fga/dot_general | solution.py:16
  95.8 5.6 %fusion.8 = f32[32,64,128]{2,0,1:T(8,128)S(1)} fusion(f32[64,160,128]{2,0,1:T(8,128)S(1)} %fusion.20, f32[160]{0:T(256)S(1)} %compare_convert_fusion, s32[160]{0:T(256)S(1)} %copy-done.4), kind=kOutput, calls=%fused_computation.11 | convolution fusion | flops 503326720 | bytes 6292736 | tf_op jit(solution)/shard_map/fgt,gd->fdt/dot_general | solution.py:21
  101.5 1.6 copy.29
  103.1 87.2 %reduce-scatter.7.cloned.1.call-done = f32[64,512]{1,0:T(8,128)} async-done(((f32[64,4096]{1,0:T(8,128)}), f32[64,512]{1,0:T(8,128)}) %reduce-scatter.7.cloned.1.call-update) | async-done | bytes 131088 | tf_op jit(solution)/shard_map/reduce_scatter | solution.py:62
  190.4 1.7 fusion.36
  192.2 59.1 %all-gather.5.cloned.1.call-done = f32[64,4096]{1,0:T(8,128)} async-done(((f32[64,512]{1,0:T(8,128)}), f32[64,4096]{1,0:T(8,128)}) %all-gather.5.cloned.1.call-update) | async-done | bytes 1048592 | tf_op jit(solution)/shard_map/all_gather | solution.py:65
  251.3 1.3 copy_bitcast_fusion.2
  252.7 3.3 gather_fusion.2
  255.9 13.9 %fusion.25 = f32[64,160,128]{2,0,1:T(8,128)S(1)} fusion(f32[160,64,128]{2,1,0:T(8,128)} %gather_fusion.2, pred[160]{0:T(512)(128)(4,1)S(1)} %compare_and_fusion, f32[160,128,128]{2,1,0:T(8,128)} %gather_fusion, pred[160]{0:T(512)(128)(4,1)S(1)} %get-tuple-element.8), kind=kOutput, calls=%fused_computation.24 | convolution fusion | flops 2017198080 | bytes 20971840 | tf_op jit(solution)/shard_map/fga,gab->fgb/dot_general | solution.py:14
  269.8 5.6 %fusion.6 = f32[32,64,128]{2,0,1:T(8,128)S(1)} fusion(f32[64,160,128]{2,0,1:T(8,128)S(1)} %fusion.25, s32[160]{0:T(256)S(1)} %copy-done.3, f32[160]{0:T(256)S(1)} %compare_convert_fusion), kind=kOutput, calls=%fused_computation.9 | convolution fusion | flops 503326720 | bytes 6292736 | tf_op jit(solution)/shard_map/fgt,gd->fdt/dot_general | solution.py:21
  275.5 1.6 copy.28
  277.1 30.8 %reduce-scatter.9.cloned.1.call-done = f32[64,512]{1,0:T(8,128)} async-done(((f32[64,4096]{1,0:T(8,128)}), f32[64,512]{1,0:T(8,128)}) %reduce-scatter.9.cloned.1.call-update) | async-done | bytes 131088 | tf_op jit(solution)/shard_map/reduce_scatter | solution.py:69
  307.9 16.4 %all_gather.11 = f32[256,512]{1,0:T(8,128)S(1)} all-gather(f32[64,512]{1,0:T(8,128)} %reduce-scatter.9.cloned.1.call-done), channel_id=1, replica_groups=mesh['row'=8,'col'=8,'rep'=4] {'rep'}, dimensions={0}, use_global_device_ids=true | all-gather | bytes 655360 | tf_op jit(solution)/shard_map/all_gather | solution.py:83
  325.7 102.4 %all-reduce.3.cloned.1.call-done = f32[64,256]{1,0:T(8,128)} async-done(((f32[64,256]{1,0:T(8,128)}), f32[64,256]{1,0:T(8,128)}) %all-reduce.3.cloned.1.call-update) | async-done | bytes 65552 | tf_op jit(solution)/shard_map/psum | solution.py:90
  428.1 2.3 fusion.37
  430.5 61.0 %all-reduce.5.cloned.1.call-done = f32[64,256]{1,0:T(8,128)} async-done(((f32[64,256]{1,0:T(8,128)}), f32[64,256]{1,0:T(8,128)}) %all-reduce.5.cloned.1.call-update) | async-done | bytes 65552 | tf_op jit(solution)/shard_map/psum | solution.py:89
  491.5 29.2 %reduce-scatter.11.cloned.1.call-done = f32[64,512]{1,0:T(8,128)} async-done(((f32[256,512]{1,0:T(8,128)}), f32[64,512]{1,0:T(8,128)}) %reduce-scatter.11.cloned.1.call-update) | async-done | bytes 131088 | tf_op jit(solution)/shard_map/reduce_scatter | solution.py:70
  520.7 1.5 copy.33
  (38 shorter events, 3.4 us)
Async XLA Ops:
  7.2 1.0 copy-start
  7.2 33.5 %reduce-scatter.5.cloned.1.call-start = ((), (), s32[]{:S(2)}) async-start(), calls=%async_computation.4 | async-start | bytes 655360 | tf_op jit(solution)/shard_map/reduce_scatter | solution.py:46
  10.5 56.4 %all-gather.3.cloned.1.call-start = ((), (), s32[]{:S(2)}) async-start(), calls=%async_computation.5 | async-start | bytes 1179648 | tf_op jit(solution)/shard_map/all_gather | solution.py:58
  40.7 149.7 %reduce-scatter.7.cloned.1.call-start = ((), (), s32[]{:S(2)}) async-start(), calls=%async_computation.6 | async-start | bytes 1179648 | tf_op jit(solution)/shard_map/reduce_scatter | solution.py:62
  42.1 14.2 %copy-start.3 = (s32[160]{0:T(256)S(1)}, s32[160]{0:T(256)}, u32[]{:S(2)}) copy-start(s32[160]{0:T(256)} %param.17) | copy-start | bytes 1924
  42.1 14.2 %copy-start.5 = (s32[160]{0:T(256)S(1)}, s32[160]{0:T(256)}, u32[]{:S(2)}) copy-start(s32[160]{0:T(256)} %param.18) | copy-start | bytes 1924
  71.5 24.3 %copy-start.4 = (s32[160]{0:T(256)S(1)}, s32[160]{0:T(256)}, u32[]{:S(2)}) copy-start(s32[160]{0:T(256)} %param.16) | copy-start | bytes 1924
  95.8 94.6 %copy-start.2 = (f32[64,512]{1,0:T(8,128)S(1)}, f32[64,512]{1,0:T(8,128)}, u32[]{:S(2)}) copy-start(f32[64,512]{1,0:T(8,128)} %param.14) | copy-start | bytes 393220
  103.1 148.2 %all-gather.5.cloned.1.call-start = ((), (), s32[]{:S(2)}) async-start(), calls=%async_computation.7 | async-start | bytes 1179648 | tf_op jit(solution)/shard_map/all_gather | solution.py:65
  192.1 115.8 %reduce-scatter.9.cloned.1.call-start = ((), (), s32[]{:S(2)}) async-start(), calls=%async_computation.8 | async-start | bytes 1179648 | tf_op jit(solution)/shard_map/reduce_scatter | solution.py:69
  269.8 54.5 %copy-start.1 = (f32[64,512]{1,0:T(8,128)S(1)}, f32[64,512]{1,0:T(8,128)}, u32[]{:S(2)}) copy-start(f32[64,512]{1,0:T(8,128)} %param.12) | copy-start | bytes 393220
  277.1 151.0 %all-reduce.3.cloned.1.call-start = ((), (), s32[]{:S(2)}) async-start(), calls=%async_computation.10 | async-start | bytes 131072 | tf_op jit(solution)/shard_map/psum | solution.py:90
  325.6 165.9 %all-reduce.5.cloned.1.call-start = ((), (), s32[]{:S(2)}) async-start(), calls=%async_computation.11 | async-start | bytes 131072 | tf_op jit(solution)/shard_map/psum | solution.py:89
  428.1 92.6 %reduce-scatter.11.cloned.1.call-start = ((), (), s32[]{:S(2)}) async-start(), calls=%async_computation.9 | async-start | bytes 655360 | tf_op jit(solution)/shard_map/reduce_scatter | solution.py:70
Sparse Core Ops, SparseCore 0:
  10.6 30.0 reduce-scatter.4
  42.5 24.2 all-gather.2
  103.2 87.1 reduce-scatter.6
  193.4 57.8 all-gather.4
  277.2 30.6 reduce-scatter.8
  325.7 102.2 all-reduce.2
  430.4 61.0 all-reduce.4
  494.6 26.0 reduce-scatter.10
